TPU v7x, 256 devices: a whole 4x4x8 slice. The times are simulated.
256 devices in a mesh: graph: 128 (over x, y, z), mp: 2 (over core).
Axes of the slice: x: 4, y: 4, z: 8, core: 2. Of those that a mesh axis runs over, the one named last changes fastest.
Arguments:
- messages: bfloat16 [131072, 512], P('graph', 'mp'), may hold values from -6 to 6
- basis_blocks: bfloat16 [12288, 128, 128], P('graph'), may hold values from -0.5 to 0.5
- source_block: int32 [12288], P('graph'), may hold values from 0 to 7
- target_owner: int32 [12288, 1], P('graph'), may hold values from 0 to 127; in each aligned block of 96 rows (0 to 95, 96 to 191, ...) at most 2 rows name the same one
- target_block: int32 [12288], P('graph'), may hold values from 0 to 7
- row_counts: int32 [12288], P('graph'), may hold values from 1 to 128
- reverse_block: int32 [1024], P('graph'), may hold values from 0 to 1023, as said below
- valid_edges: int32 [128], P('graph'), may hold values from 512 to 1024
- weight_in: bfloat16 [3, 512, 512], P(None, None, 'mp'), may hold values from -0.25 to 0.25
- weight_out: bfloat16 [3, 512, 512], P(None, 'mp'), may hold values from -0.25 to 0.25
Outputs:
- updated: bfloat16 [131072, 512], P('graph', 'mp')
Inputs may be any that keep to these rules, and one draw needn't show every extreme that they name: `target_owner`: among the 96 triplet blocks of one device, no owner is named more than 2 times, a bound that some block reaches. `reverse_block`: an involution on edge blocks. Of device g's 8 blocks, the first 2 pair with blocks 2 to 3 of device (g - 1) mod 128, blocks 2 to 3 pair with the first 2 of device (g + 1) mod 128, and the others pair with blocks of device g itself.
All inputs are finite; a program needn't handle non-finite values.
Results may differ from a plain program's by a relative error of at most 0.0073.
Values may be sent and summed in bfloat16 or wider, within the bound.
A program may use at most 128 MiB of HBM per device.

v0:
```python
import jax
import jax.numpy as jnp
from jax import lax
from jax.sharding import PartitionSpec as P

MLPS = 3
BLK = 128


pair_scale = 0.7071067811865476


def padded_2(array, sides, width):
    for axis, dim in sides:
        size, length = (lax.axis_size(axis), array.shape[dim])
        up = [(i, (i + 1) % size) for i in range(size)]
        down = [(j, i) for i, j in up]
        last = lax.slice_in_dim(array, length - width, length, axis=dim)
        leading = lax.slice_in_dim(array, 0, width, axis=dim)
        before = lax.ppermute(last, axis, up)
        after = lax.ppermute(leading, axis, down)
        array = jnp.concatenate([before, array, after], axis=dim)
    return array


def place_slots(values, place, devices, capacity):
    shape_rest = values.shape[1:]
    padded = jnp.zeros((devices * capacity,) + shape_rest, values.dtype).at[place].set(values)
    return padded.reshape((devices, capacity) + shape_rest)


def sum_into_blocks(incoming, arrived, blocks):
    count_all = arrived.shape[0]
    rows, cols = (incoming.shape[1], incoming.shape[2])
    selector = (jnp.arange(blocks, dtype=jnp.int32)[:, None] == arrived[None, :]).astype(
        jnp.bfloat16
    )
    summed = jnp.dot(
        selector, incoming.reshape(count_all, rows * cols), preferred_element_type=jnp.float32
    )
    return summed.reshape(blocks, rows, cols)


def masked_products(basis_rows, source_data, own_rows, counts):
    products = jnp.einsum(
        "str,src->stc", basis_rows, source_data, preferred_element_type=jnp.float32
    )
    keep = own_rows[None, :] < counts[:, None]
    return jnp.where(keep[:, :, None], products, 0.0).astype(jnp.bfloat16)


def reverse_pairs(combined, reverse_block, this_device, devices, blocks, border):
    leading = combined[: 2 * border]
    extended = padded_2(leading, (("graph", 0),), border)
    lower_rim = extended[:border]
    upper_rim = extended[3 * border :]
    full = jnp.concatenate([lower_rim, combined, upper_rim], axis=0)
    holder = reverse_block // blocks
    within = reverse_block % blocks
    before = (this_device - 1) % devices
    local_index = jnp.where(
        holder == this_device,
        border + within,
        jnp.where(holder == before, within - border, border + blocks + within),
    )
    return full[local_index]


def local(
    messages,
    basis_blocks,
    source_block,
    target_owner,
    target_block,
    row_counts,
    reverse_block,
    valid_edges,
    weight_in,
    weight_out,
):
    devices = lax.axis_size("graph")
    this_device = lax.axis_index("graph")
    edge_rows, part_width = messages.shape
    blocks = edge_rows // BLK
    slots = source_block.shape[0]
    capacity = max(2, (slots + devices - 1) // devices + 1)
    border = blocks // 4
    owners = target_owner[:, 0]
    slot_index = jnp.arange(slots, dtype=jnp.int32)
    same_owner = (owners[:, None] == owners[None, :]) & (slot_index[None, :] < slot_index[:, None])
    earlier = jnp.sum(same_owner.astype(jnp.int32), axis=1)
    place = owners * capacity + earlier
    row_share = BLK
    own_rows = jnp.arange(BLK, dtype=jnp.int32)
    local_rows = messages.reshape(blocks, BLK, part_width)
    source_data = local_rows[source_block]
    products = masked_products(basis_blocks, source_data, own_rows, row_counts)
    out_products = place_slots(products, place, devices, capacity)
    out_labels = place_slots(target_block, place, devices, capacity)
    incoming, arrived = (
        lax.all_to_all(out_products, "graph", split_axis=0, concat_axis=0, tiled=True),
        lax.all_to_all(out_labels, "graph", split_axis=0, concat_axis=0, tiled=True),
    )
    arrived_count = devices * capacity
    aggregate = sum_into_blocks(
        incoming.reshape((arrived_count,) + incoming.shape[2:]), arrived.reshape(-1), blocks
    )
    combined = (local_rows.astype(jnp.float32) + aggregate).astype(jnp.bfloat16)
    swapped = reverse_pairs(combined, reverse_block, this_device, devices, blocks, border)
    state = (combined.astype(jnp.float32) + swapped.astype(jnp.float32)) * pair_scale
    width_here = state.shape[2]
    state = state.reshape(blocks * row_share, width_here)
    position = (jnp.arange(blocks, dtype=jnp.int32)[:, None] * BLK + own_rows[None, :]).reshape(-1)
    keep_edge = position < valid_edges[0]
    for layer in range(MLPS):
        layer_input = lax.all_gather(state.astype(jnp.bfloat16), "mp", axis=1, tiled=True)
        hidden = jax.nn.silu(
            jnp.dot(layer_input, weight_in[layer], preferred_element_type=jnp.float32)
        ).astype(jnp.bfloat16)
        partial_sum = jnp.dot(hidden, weight_out[layer], preferred_element_type=jnp.float32)
        state = state + lax.psum_scatter(partial_sum, "mp", scatter_dimension=1, tiled=True)
    return jnp.where(keep_edge[:, None], state, 0.0).astype(jnp.bfloat16)


def solution(mesh):
    in_specs = (
        P("graph", "mp"),
        P("graph", None, None),
        P("graph"),
        P("graph", None),
        P("graph"),
        P("graph"),
        P("graph"),
        P("graph"),
        P(None, None, "mp"),
        P(None, "mp", None),
    )
    out_specs = P("graph", "mp")
    return jax.shard_map(local, mesh=mesh, in_specs=in_specs, out_specs=out_specs, check_vma=False)
```

profile of v0, /device:TPU:1, one launch (start us, length us, event | category | flops | bytes accessed | tf_op | source)
XLA Modules:
  0.0 636.1 jit_solution(6905696760850788249)
XLA Ops:
  6.5 0.0 copy-start
  6.5 1.0 convert_reduce_fusion
  7.5 0.7 fusion.45
  8.2 1.0 scatter_custom_fusion
  9.2 0.8 all_to_all.9
  10.0 16.3 %all-to-all-start = ((s32[128,1,2]{2,1,0:T(1,128)}), s32[128,1,2]{2,1,0:T(1,128)S(1)}, u32[]{:S(2)}, u32[]{:S(2)}) async-start(s32[128,1,2]{2,1,0:T(1,128)} %bitcast.6), calls=%async_computation | async-start | bytes 131072 | tf_op jit(solution)/shard_map/all_to_all | solution.py:102
  26.3 0.7 iota_compare_fusion
  27.1 0.7 compare_select_fusion.1
  27.7 7.0 %gather_fusion = bf16[96,128,256]{2,1,0:T(8,128)(2,1)} fusion(bf16[8,128,256]{2,1,0:T(8,128)(2,1)} %bitcast.73, s32[1024]{0:T(1024)S(1)} %pad_clamp_fusion.1), kind=kCustom, calls=%fused_computation | custom fusion | bytes 12583296 | tf_op jit(solution)/shard_map/gather | solution.py:96
  34.7 0.0 copy-done
  34.7 7.8 %fusion = bf16[96,128,256]{1,2,0:T(8,128)(2,1)} fusion(pred[96,128]{1,0:T(8,128)(4,1)S(1)} %iota_compare_fusion, bf16[96,128,256]{2,1,0:T(8,128)(2,1)} %gather_fusion, bf16[96,128,128]{2,1,0:T(8,128)(2,1)S(1)} %copy-done), kind=kOutput, calls=%fused_computation.5 | convolution fusion | flops 811597824 | bytes 15740928 | tf_op jit(solution)/shard_map/str,src->stc/dot_general | solution.py:45
  42.5 8.6 %copy.32 = bf16[96,128,256]{2,1,0:T(8,128)(2,1)} copy(bf16[96,128,256]{1,2,0:T(8,128)(2,1)} %fusion) | data formatting | bytes 12582912 | tf_op jit(solution)/shard_map/convert_element_type | solution.py:49
  51.2 6.0 broadcast_in_dim.49
  57.1 17.8 %scatter_fusion = bf16[256,128,256]{2,1,0:T(8,128)(2,1)} fusion(bf16[256,128,256]{2,1,0:T(8,128)(2,1)} %broadcast_in_dim.49, s32[96]{0:T(128)S(1)} %fusion.45, bf16[96,128,256]{2,1,0:T(8,128)(2,1)} %copy.32), kind=kCustom, calls=%fused_computation.3 | custom fusion | bytes 18874752 | tf_op jit(solution)/shard_map/scatter | solution.py:28
  74.9 0.0 all-to-all-done
  74.9 13.8 %all-to-all-start.1 = ((bf16[128,2,128,256]{3,2,1,0:T(8,128)(2,1)}), bf16[128,2,128,256]{3,2,1,0:T(8,128)(2,1)}, u32[]{:S(2)}, u32[]{:S(2)}) async-start(bf16[128,2,128,256]{3,2,1,0:T(8,128)(2,1)} %bitcast.72), calls=%async_computation.1 | async-start | bytes 33554432 | tf_op jit(solution)/shard_map/all_to_all | solution.py:101
  88.7 0.2 all-gather.4.cloned.1.call-start
  89.0 0.5 broadcast.110
  89.5 0.8 reduce.3
  90.3 0.1 eq.51
  90.4 364.2 %all-to-all-done.1 = bf16[128,2,128,256]{3,2,1,0:T(8,128)(2,1)} async-done(((bf16[128,2,128,256]{3,2,1,0:T(8,128)(2,1)}), bf16[128,2,128,256]{3,2,1,0:T(8,128)(2,1)}, u32[]{:S(2)}, u32[]{:S(2)}) %all-to-all-start.1) | async-done | bytes 16777248 | tf_op jit(solution)/shard_map/all_to_all | solution.py:101
  454.6 17.8 %copy.38 = bf16[32,8,128,256]{3,1,2,0:T(8,128)(2,1)} copy(bf16[32,8,128,256]{3,2,1,0:T(8,128)(2,1)} %bitcast.20) | data formatting | bytes 33554432
  472.4 22.3 %copy.33 = bf16[32768,256]{1,0:T(8,128)(2,1)} copy(bf16[32768,256]{0,1:T(8,128)(2,1)} %bitcast.76) | data formatting | bytes 33554432 | tf_op jit(solution)/shard_map/dot_general | solution.py:38
  494.7 0.0 copy-done.2
  494.7 10.2 %fusion.1 = bf16[8,128,256]{2,0,1:T(8,128)(2,1)S(1)} fusion(bf16[128,256,256]{2,1,0:T(8,128)(2,1)} %bitcast.75, bf16[8,128,256]{2,1,0:T(8,128)(2,1)S(1)} %bitcast.74, s32[256]{0:T(256)S(1)} %eq.51), kind=kOutput, calls=%fused_computation.7 | convolution fusion | flops 135006208 | bytes 17826816 | tf_op jit(solution)/shard_map/dot_general | solution.py:38
  504.9 0.2 fusion.52
  505.1 1.5 collective-permute-start.1
  506.6 0.0 collective-permute-start
  506.7 0.0 copy-done.5
  506.7 2.3 collective-permute-done.1
  509.0 6.9 %collective-permute-done = bf16[2,128,256]{2,0,1:T(2,128)(2,1)S(1)} collective-permute-done((bf16[2,128,256]{2,0,1:T(2,128)(2,1)S(1)}, bf16[2,128,256]{2,0,1:T(2,128)(2,1)S(1)}, u32[]{:S(2)}, u32[]{:S(2)}) %collective-permute-start) | collective-permute-done | bytes 131104 | tf_op jit(solution)/shard_map/ppermute | solution.py:20
  515.9 0.6 pad_maximum_fusion
  516.5 0.2 copy.34
  516.8 0.6 gather_fusion.1
  517.3 0.4 add_multiply_fusion
  517.8 0.3 copy.36
  518.1 0.9 bitcast_convert_fusion
  519.0 0.0 all-gather.4.cloned.1.call-update
  519.1 0.0 reduce-scatter.4.cloned.1.call-start
  519.1 10.8 %all-gather.4.cloned.1.call-done = bf16[1024,512]{1,0:T(8,128)(2,1)} async-done(((bf16[1024,256]{1,0:T(8,128)(2,1)}), bf16[1024,512]{1,0:T(8,128)(2,1)}) %all-gather.4.cloned.1.call-update) | async-done | bytes 1048592 | tf_op jit(solution)/shard_map/all_gather | solution.py:116
  529.9 3.8 fusion.2
  533.7 0.0 reduce-scatter.4.cloned.1.call-update
  533.7 0.0 all-gather.6.cloned.1.call-start
  533.8 16.1 %reduce-scatter.4.cloned.1.call-done = f32[1024,256]{1,0:T(8,128)} async-done(((f32[1024,512]{1,0:T(8,128)}), f32[1024,256]{1,0:T(8,128)}) %reduce-scatter.4.cloned.1.call-update) | async-done | bytes 1048592 | tf_op jit(solution)/shard_map/reduce_scatter | solution.py:121
  549.8 2.2 fusion.9
  552.0 0.0 all-gather.6.cloned.1.call-update
  552.1 0.0 reduce-scatter.6.cloned.1.call-start
  552.1 15.9 %all-gather.6.cloned.1.call-done = bf16[1024,512]{1,0:T(8,128)(2,1)} async-done(((bf16[1024,256]{1,0:T(8,128)(2,1)}), bf16[1024,512]{1,0:T(8,128)(2,1)}) %all-gather.6.cloned.1.call-update) | async-done | bytes 1048592 | tf_op jit(solution)/shard_map/all_gather | solution.py:116
  568.1 3.8 fusion.3
  571.8 0.0 reduce-scatter.6.cloned.1.call-update
  571.9 0.0 all-gather.8.cloned.1.call-start
  571.9 16.1 %reduce-scatter.6.cloned.1.call-done = f32[1024,256]{1,0:T(8,128)} async-done(((f32[1024,512]{1,0:T(8,128)}), f32[1024,256]{1,0:T(8,128)}) %reduce-scatter.6.cloned.1.call-update) | async-done | bytes 1048592 | tf_op jit(solution)/shard_map/reduce_scatter | solution.py:121
  588.0 0.0 copy-done.4
  588.0 2.2 fusion.51
  590.2 0.0 all-gather.8.cloned.1.call-update
  590.2 0.0 copy-start.1
  590.2 0.0 reduce-scatter.8.cloned.1.call-start
  590.3 15.9 %all-gather.8.cloned.1.call-done = bf16[1024,512]{1,0:T(8,128)(2,1)} async-done(((bf16[1024,256]{1,0:T(8,128)(2,1)}), bf16[1024,512]{1,0:T(8,128)(2,1)}) %all-gather.8.cloned.1.call-update) | async-done | bytes 1048592 | tf_op jit(solution)/shard_map/all_gather | solution.py:116
  606.2 3.8 fusion.4
  610.0 0.0 reduce-scatter.8.cloned.1.call-update
  610.7 0.1 fusion.44
  610.7 15.4 %reduce-scatter.8.cloned.1.call-done = f32[1024,256]{1,0:T(8,128)} async-done(((f32[1024,512]{1,0:T(8,128)}), f32[1024,256]{1,0:T(8,128)}) %reduce-scatter.8.cloned.1.call-update) | async-done | bytes 1048592 | tf_op jit(solution)/shard_map/reduce_scatter | solution.py:121
  626.1 3.2 select_convert_fusion.1
  629.3 0.0 copy-done.1
  (9 shorter events, 0.0 us)
Async XLA Ops:
  6.5 28.2 %copy-start = (bf16[96,128,128]{2,1,0:T(8,128)(2,1)S(1)}, bf16[96,128,128]{2,1,0:T(8,128)(2,1)}, u32[]{:S(2)}) copy-start(bf16[96,128,128]{2,1,0:T(8,128)(2,1)} %param.11) | copy-start | bytes 9437188
  10.0 64.9 %all-to-all-start = ((s32[128,1,2]{2,1,0:T(1,128)}), s32[128,1,2]{2,1,0:T(1,128)S(1)}, u32[]{:S(2)}, u32[]{:S(2)}) async-start(s32[128,1,2]{2,1,0:T(1,128)} %bitcast.6), calls=%async_computation | async-start | bytes 131072 | tf_op jit(solution)/shard_map/all_to_all | solution.py:102
  74.9 379.7 %all-to-all-start.1 = ((bf16[128,2,128,256]{3,2,1,0:T(8,128)(2,1)}), bf16[128,2,128,256]{3,2,1,0:T(8,128)(2,1)}, u32[]{:S(2)}, u32[]{:S(2)}) async-start(bf16[128,2,128,256]{3,2,1,0:T(8,128)(2,1)} %bitcast.72), calls=%async_computation.1 | async-start | bytes 33554432 | tf_op jit(solution)/shard_map/all_to_all | solution.py:101
  88.7 441.2 %all-gather.4.cloned.1.call-start = ((), (), s32[]{:S(2)}) async-start(), calls=%async_computation.5 | async-start | bytes 1572864 | tf_op jit(solution)/shard_map/all_gather | solution.py:116
  472.4 22.3 %copy-start.2 = (bf16[1024,256]{1,0:T(8,128)(2,1)S(1)}, bf16[1024,256]{1,0:T(8,128)(2,1)}, u32[]{:S(2)}) copy-start(bf16[1024,256]{1,0:T(8,128)(2,1)} %param.10) | copy-start | bytes 1572868
  494.7 12.0 %copy-start.5 = (s32[8]{0:T(128)S(1)}, s32[8]{0:T(128)}, u32[]{:S(2)}) copy-start(s32[8]{0:T(128)} %param.16) | copy-start | bytes 100
  505.1 3.9 collective-permute-start.1
  506.6 9.2 %collective-permute-start = (bf16[2,128,256]{2,0,1:T(2,128)(2,1)S(1)}, bf16[2,128,256]{2,0,1:T(2,128)(2,1)S(1)}, u32[]{:S(2)}, u32[]{:S(2)}) collective-permute-start(bf16[2,128,256]{2,0,1:T(2,128)(2,1)S(1)} %get-tuple-element.5), channel_id=1, source_target_pairs={{0,2},{2,4},{4,6},{6,8},{8,10},{10,12},{12,14},{14,16},{16,18},{18... | collective-permute-start | bytes 393224 | tf_op jit(solution)/shard_map/ppermute | solution.py:20
  518.1 69.9 %copy-start.3 = (f32[8,128,256]{2,1,0:T(8,128)}, f32[8,128,256]{2,1,0:T(8,128)S(1)}, u32[]{:S(2)}) copy-start(f32[8,128,256]{2,1,0:T(8,128)S(1)} %copy.36) | copy-start | bytes 3145732
  519.1 30.7 %reduce-scatter.4.cloned.1.call-start = ((), (), s32[]{:S(2)}) async-start(), calls=%async_computation.6 | async-start | bytes 3145728 | tf_op jit(solution)/shard_map/reduce_scatter | solution.py:121
  533.7 34.4 %all-gather.6.cloned.1.call-start = ((), (), s32[]{:S(2)}) async-start(), calls=%async_computation.7 | async-start | bytes 1572864 | tf_op jit(solution)/shard_map/all_gather | solution.py:116
  549.8 38.2 %copy-start.4 = (f32[1024,256]{1,0:T(8,128)S(1)}, f32[1024,256]{1,0:T(8,128)}, u32[]{:S(2)}) copy-start(f32[1024,256]{1,0:T(8,128)} %reduce-scatter.4.cloned.1.call-done) | copy-start | bytes 3145732
  552.1 35.9 %reduce-scatter.6.cloned.1.call-start = ((), (), s32[]{:S(2)}) async-start(), calls=%async_computation.8 | async-start | bytes 3145728 | tf_op jit(solution)/shard_map/reduce_scatter | solution.py:121
  571.9 34.3 %all-gather.8.cloned.1.call-start = ((), (), s32[]{:S(2)}) async-start(), calls=%async_computation.9 | async-start | bytes 1572864 | tf_op jit(solution)/shard_map/all_gather | solution.py:116
  590.2 39.1 %copy-start.1 = (bf16[96,128,128]{2,1,0:T(8,128)(2,1)S(1)}, bf16[96,128,128]{2,1,0:T(8,128)(2,1)}, u32[]{:S(2)}) copy-start(bf16[96,128,128]{2,1,0:T(8,128)(2,1)} %param.11) | copy-start | bytes 9437188
  590.2 35.9 %reduce-scatter.8.cloned.1.call-start = ((), (), s32[]{:S(2)}) async-start(), calls=%async_computation.10 | async-start | bytes 3145728 | tf_op jit(solution)/shard_map/reduce_scatter | solution.py:121
Sparse Core Ops, SparseCore 0:
  519.2 10.6 all-gather.3
  533.8 15.9 reduce-scatter.3
  552.2 15.8 all-gather.5
  572.0 15.9 reduce-scatter.5
  590.3 15.8 all-gather.7
  610.1 15.9 reduce-scatter.7
where the time goes:
time: 638 us; the launch traced here: 636 us
  waiting for transfers between devices  464 us (73%)
  local copies, waits for them, and re-layouts  83.3 us (13%)
  starting transfers between devices  32.1 us (5%)
  matrix products  29.3 us (5%)
  between operations  14.3 us (2%)
  other arithmetic  13.6 us (2%)
    all_to_all x1, waiting for transfers between devices, local(): lax.all_to_all(out_products, 'graph', split_axis=0, concat_axis=0, tiled=...  364 us
    reduce_scatter x3, waiting for transfers between devices, local(): lax.psum_scatter(partial_sum, 'mp', scatter_dimension=1, tiled=True)  47.5 us
    all_gather x3, waiting for transfers between devices, local(): lax.all_gather(state.astype(jnp.bfloat16), 'mp', axis=1, tiled=True)  42.6 us
    dot_general x1, local copies, waits for them, and re-layouts, sum_into_blocks(): jnp.dot(selector, incoming.reshape(count_all, rows * cols), preferred_ele...  22.3 us
    scatter x2, local copies, waits for them, and re-layouts, place_slots(): jnp.zeros((devices * capacity,) + shape_rest, values.dtype).at[place]  18.8 us
    unnamed x13, local copies, waits for them, and re-layouts  17.8 us
    all_to_all x1, starting transfers between devices, local(): lax.all_to_all(out_labels, 'graph', split_axis=0, concat_axis=0, tiled=True)  16.3 us
    all_to_all x1, starting transfers between devices, local(): lax.all_to_all(out_products, 'graph', split_axis=0, concat_axis=0, tiled=...  13.8 us
  transfers between devices with their start and end apart: 10, of which 9 were waited for; matrix products, arithmetic and copies ran while one was open for 8% of the time, Pallas kernels for 0%

commit v1 on v0

v1 whole, which is shorter than its diff:
```python
import functools

import jax
import jax.numpy as jnp
from jax import lax
from jax.experimental import pallas as pl
from jax.experimental.pallas import tpu as pltpu
from jax.sharding import PartitionSpec as P

BLK = 128
MLPS = 3
NX, NY, NZ = 4, 4, 8
PLANE = NX * NY
EB = 8
SLOTS = 96
SCALE = 0.7071067811865476
MESH = pl.DeviceIdType.MESH
VMEM = pltpu.VMEM
SMEM = pltpu.SMEM


def coords():
    g = lax.axis_index("graph")
    return g, g // (NY * NZ), (g // NZ) % NY, g % NZ, lax.axis_index("mp")


def slot_kernel(core_ref, owner_ref, source_ref, target_ref, count_ref, basis_ref, out_ref, meta_ref, used):
    c = core_ref[0]
    out_ref[...] = jnp.zeros_like(out_ref)

    def clear(i, _):
        used[i] = 0
        meta_ref[i // 8, 0, (i % 8) * 2] = 0
        meta_ref[i // 8, 0, (i % 8) * 2 + 1] = 0
        return 0

    lax.fori_loop(0, PLANE * NZ, clear, 0)
    row = lax.broadcasted_iota(jnp.int32, (BLK, BLK), 0)

    def place(t, _):
        o = owner_ref[t]
        k = used[o]
        used[o] = k + 1
        meta_ref[o // 8, 0, (o % 8) * 2 + k] = target_ref[t] * 8 + source_ref[t]

        @pl.when(k == c)
        def _():
            out_ref[o] = jnp.where(row < count_ref[t], basis_ref[t].astype(jnp.float32), 0.0).astype(jnp.bfloat16)

        return 0

    lax.fori_loop(0, SLOTS, place, 0)


def slot_blocks(core, owner, source, target, count, basis):
    smem = pl.BlockSpec(memory_space=SMEM)
    return pl.pallas_call(
        slot_kernel,
        out_shape=(
            jax.ShapeDtypeStruct((PLANE * NZ, BLK, BLK), jnp.bfloat16),
            jax.ShapeDtypeStruct((PLANE, 8, 128), jnp.int32),
        ),
        in_specs=[smem] * 5 + [pl.BlockSpec(memory_space=VMEM)],
        out_specs=(pl.BlockSpec(memory_space=VMEM), smem),
        scratch_shapes=[SMEM((PLANE * NZ,), jnp.int32)],
        name="slots",
    )(core, owner, source, target, count, basis)


def plane_kernel(msg, pb, meta, G, BB, MT, msg_s, msg_r, bas_s, bas_r, fwd_s, fwd_r, met_s, met_r, loc):
    g, x, y, z, c = coords()
    me = x * NY + y
    half, quarter = 512, 256

    def pos(dx, dy):
        return ((x + dx) % NX) * NY + (y + dy) % NY

    def dev(dx, dy):
        return (pos(dx, dy) * NZ + z, c)

    partner = (g, 1 - c)
    others = [(dx, dy) for dx in range(NX) for dy in range(NY) if (dx, dy) != (0, 0)]
    barrier = pltpu.get_barrier_semaphore()
    for d in others:
        pl.semaphore_signal(barrier, inc=1, device_id=dev(*d), device_id_type=MESH)
    pl.semaphore_signal(barrier, inc=1, device_id=partner, device_id_type=MESH)
    pl.semaphore_wait(barrier, len(others) + 1)

    def local_copy(src, dst, i):
        return pltpu.make_async_copy(src, dst, loc.at[i])

    own = [
        local_copy(msg, G.at[me], 0),
        local_copy(pb.at[pl.ds(me * NZ, NZ)], BB.at[c, me], 1),
        local_copy(meta.at[me], MT.at[me], 2),
    ]
    for cp in own:
        cp.start()

    def remote(src, dst, s, r, i, device):
        return pltpu.make_async_remote_copy(
            src_ref=src, dst_ref=dst, send_sem=s.at[i], recv_sem=r.at[i], device_id=device, device_id_type=MESH
        )

    def ab(h, a, b):
        return (a, b) if h == 0 else (b, a)

    def piece(h, a, b, part):
        p = pos(*ab(h, a, b))
        rows = {None: (h * half, half), 0: (h * half, quarter), 1: (h * half + quarter, quarter)}[part]
        return p, pl.ds(rows[0], rows[1])

    def gref(h, a, b, part):
        p, rows = piece(h, a, b, part)
        return G.at[p, rows]

    roles = {}
    sems = {}
    for h in (0, 1):
        for name in ["a1+", "a1-", "a2+", "a2-"] + [n + str(a) for n in ("b1+", "b1-", "b2+", "b2-") for a in (0, 1, 2, 3)]:
            sems[h, name] = len(sems)

    def message(h, name, sending):
        sign = 1 if name[2] == "+" else -1
        if name[:2] == "a1":
            a, b, part, step = 0, 0, None, (sign, 0)
        elif name[:2] == "a2":
            a, b, part, step = -sign, 0, (0 if sign > 0 else 1), (sign, 0)
        elif name[:2] == "b1":
            a, b, part, step = int(name[3]), 0, None, (0, sign)
        else:
            a, b, part, step = int(name[3]), -sign, (0 if sign > 0 else 1), (0, sign)
        if a % 4 == 0 and b == 0:
            src = msg.at[piece(h, 0, 0, part)[1]]
        else:
            src = gref(h, a, b, part)
        if not sending:
            src = gref(h, a - step[0], b - step[1], part)
            return remote(src, src, msg_s, msg_r, sems[h, name], dev(*ab(h, *step)))
        return remote(src, gref(h, a, b, part), msg_s, msg_r, sems[h, name], dev(*ab(h, *step)))

    started = []

    def send(h, name):
        cp = message(h, name, True)
        cp.start()
        started.append(cp)

    def recv(h, name):
        message(h, name, False).wait_recv()

    def basis_send(i):
        d = others[i]
        p = pos(*d)
        cp = remote(pb.at[pl.ds(p * NZ, NZ)], BB.at[c, me], bas_s, bas_r, i, dev(*d))
        cp.start()
        started.append(cp)

    def basis_forward(i):
        d = others[i]
        p = pos(-d[0], -d[1])
        there = BB.at[c, p]
        remote(there, there, bas_s, bas_r, i, dev(*d)).wait_recv()
        cp = remote(there, there, fwd_s, fwd_r, i, partner)
        cp.start()
        started.append(cp)

    for h in (0, 1):
        send(h, "a1+")
        send(h, "a1-")
    for h in (0, 1):
        send(h, "b1+0")
        send(h, "b1-0")
    for i, d in enumerate(others):
        cp = remote(meta.at[pos(*d)], MT.at[me], met_s, met_r, i, dev(*d))
        cp.start()
        started.append(cp)
    cp = remote(pb.at[pl.ds(me * NZ, NZ)], BB.at[c, me], fwd_s, fwd_r, len(others), partner)
    cp.start()
    started.append(cp)
    order = sorted(range(len(others)), key=lambda i: sum(min(v, 4 - v) for v in others[i]))
    for i in order[:5]:
        basis_send(i)
    for h in (0, 1):
        recv(h, "a1+")
        send(h, "a2+")
        send(h, "b1+3")
        send(h, "b1-3")
        recv(h, "a1-")
        send(h, "a2-")
        send(h, "b1+1")
        send(h, "b1-1")
    for i in order[5:10]:
        basis_send(i)
    for h in (0, 1):
        recv(h, "b1+0")
        send(h, "b2+0")
        recv(h, "b1-0")
        send(h, "b2-0")
    for h in (0, 1):
        recv(h, "a2+")
        recv(h, "a2-")
        send(h, "b1+2")
        send(h, "b1-2")
    for i in order[10:]:
        basis_send(i)
    for a in ("3", "1"):
        for h in (0, 1):
            recv(h, "b1+" + a)
            send(h, "b2+" + a)
            recv(h, "b1-" + a)
            send(h, "b2-" + a)
    for i in order[:5]:
        basis_forward(i)
    for h in (0, 1):
        recv(h, "b1+2")
        send(h, "b2+2")
        recv(h, "b1-2")
        send(h, "b2-2")
    for i in order[5:]:
        basis_forward(i)
    for a in ("0", "3", "1", "2"):
        for h in (0, 1):
            recv(h, "b2+" + a)
            recv(h, "b2-" + a)
    for i, d in enumerate(others):
        there = BB.at[1 - c, pos(-d[0], -d[1])]
        remote(there, there, fwd_s, fwd_r, i, partner).wait_recv()
        slot = MT.at[pos(-d[0], -d[1])]
        remote(slot, slot, met_s, met_r, i, dev(*d)).wait_recv()
    there = BB.at[1 - c, me]
    remote(there, there, fwd_s, fwd_r, len(others), partner).wait_recv()
    for cp in own:
        cp.wait()
    for cp in started:
        cp.wait_send()


def plane_exchange(messages, basis, meta):
    n = PLANE - 1
    any_ = pl.BlockSpec(memory_space=pl.ANY)
    dma = pltpu.SemaphoreType.DMA
    return pl.pallas_call(
        plane_kernel,
        out_shape=(
            jax.ShapeDtypeStruct((PLANE,) + messages.shape, jnp.bfloat16),
            jax.ShapeDtypeStruct((2, PLANE, NZ, BLK, BLK), jnp.bfloat16),
            jax.ShapeDtypeStruct((PLANE, 8, 128), jnp.int32),
        ),
        in_specs=[pl.BlockSpec(memory_space=VMEM)] * 2 + [any_],
        out_specs=(any_,) * 3,
        scratch_shapes=[
            dma((40,)), dma((40,)), dma((n,)), dma((n,)), dma((n + 1,)), dma((n + 1,)), dma((n,)), dma((n,)), dma((3,)),
        ],
        compiler_params=pltpu.CompilerParams(collective_id=0, has_side_effects=True),
        name="plane",
    )(messages, basis, meta)


def product_kernel(meta, g_ref, b_ref, out_ref, acc):
    p = pl.program_id(0)

    @pl.when(p == 0)
    def _():
        acc[...] = jnp.zeros_like(acc)

    def owner(zo, _):
        for k in (0, 1):
            m = meta[p, 0, zo * 2 + k]
            prod = jnp.dot(b_ref[k, 0, zo], g_ref[0, m % 8], preferred_element_type=jnp.float32)
            t = zo * EB + m // 8
            acc[t] = acc[t] + prod
        return 0

    lax.fori_loop(0, NZ, owner, 0)

    @pl.when(p == PLANE - 1)
    def _():
        def put(t, _):
            out_ref[t] = acc[t].astype(jnp.bfloat16)
            return 0

        lax.fori_loop(0, NZ * EB, put, 0)


def plane_products(meta, gathered, basis):
    width = gathered.shape[-1]
    return pl.pallas_call(
        product_kernel,
        out_shape=jax.ShapeDtypeStruct((NZ * EB, BLK, width), jnp.bfloat16),
        grid=(PLANE,),
        in_specs=[
            pl.BlockSpec(memory_space=SMEM),
            pl.BlockSpec((1, EB, BLK, width), lambda p: (p, 0, 0, 0)),
            pl.BlockSpec((2, 1, NZ, BLK, BLK), lambda p: (0, p, 0, 0, 0)),
        ],
        out_specs=pl.BlockSpec((NZ * EB, BLK, width), lambda p: (0, 0, 0)),
        scratch_shapes=[VMEM((NZ * EB, BLK, width), jnp.float32)],
        name="products",
    )(meta, gathered.reshape(PLANE, EB, BLK, width), basis)


def tail_kernel(
    rev, valid, part, msg, w_in, w_out, out,
    up_s, dn_s, up_r, dn_r, full, st, give, win2, wout2, hid, res, fin,
    z_s, z_r, rim_s, rim_r, mp_s, mp_r,
):
    g, x, y, z, c = coords()
    base = g - z
    up_dev = (base + (z + 1) % NZ, c)
    dn_dev = (base + (z + NZ - 1) % NZ, c)
    count = NX * NY * NZ
    before, after = (g + count - 1) % count, (g + 1) % count
    partner = (g, 1 - c)
    barrier = pltpu.get_barrier_semaphore()
    for d in (up_dev, dn_dev, (before, c), (after, c), partner):
        pl.semaphore_signal(barrier, inc=1, device_id=d, device_id_type=MESH)
    pl.semaphore_wait(barrier, 5)

    def remote(src, dst, s, r, i, device):
        return pltpu.make_async_remote_copy(
            src_ref=src, dst_ref=dst, send_sem=s.at[i], recv_sem=r.at[i], device_id=device, device_id_type=MESH
        )

    started = []

    def go(*args):
        cp = remote(*args)
        cp.start()
        started.append(cp)

    def chain(up, s, q):
        return (0 if up else 8) + s * 2 + q

    def blocks(q):
        return pl.ds(q * 4, 4)

    def part_of(up, s, q):
        zo = (z + 4 - s) % NZ if up else (z + 4 + s) % NZ
        return zo * EB + q * 4

    first = {True: 0, False: 1}
    recv_buf = {True: up_r, False: dn_r}
    send_buf = {True: up_s, False: dn_s}
    dest = {True: up_dev, False: dn_dev}

    def z_send(up, s, q, src):
        go(src, recv_buf[up].at[s, blocks(q)], z_s, z_r, chain(up, s, q), dest[up])

    def z_wait(up, s, q):
        there = recv_buf[up].at[s, blocks(q)]
        remote(there, there, z_s, z_r, chain(up, s, q), dest[up]).wait_recv()

    for up in (True, False):
        z_send(up, 0, first[up], part.at[pl.ds(part_of(up, 0, first[up]), 4)])
    for up in (True, False):
        q = 1 - first[up]
        z_send(up, 1, q, part.at[pl.ds(part_of(up, 1, q), 4)])
    go(w_in, win2, mp_s, mp_r, 0, partner)
    go(w_out, wout2, mp_s, mp_r, 1, partner)
    for s in (1, 2, 3):
        for q0 in (0, 1):
            for up in (True, False):
                q = first[up] if q0 == 0 else 1 - first[up]
                if s == 1 and q != first[up]:
                    continue
                z_wait(up, s - 1, q)

                def add(i, _, up=up, s=s, q=q):
                    b = q * 4 + i
                    send_buf[up][s, b] = (
                        part[part_of(up, s, q) + i].astype(jnp.float32) + recv_buf[up][s - 1, b].astype(jnp.float32)
                    ).astype(jnp.bfloat16)
                    return 0

                lax.fori_loop(0, 4, add, 0)
                z_send(up, s, q, send_buf[up].at[s, blocks(q)])
    for q in (0, 1):
        z_wait(True, 3, q)
        z_wait(False, 3, q)

        def finish(i, _, q=q):
            b = q * 4 + i
            total = part[z * EB + b].astype(jnp.float32) + up_r[3, b].astype(jnp.float32) + dn_r[3, b].astype(jnp.float32)
            full[2 + b] = (msg[b].astype(jnp.float32) + total).astype(jnp.bfloat16)
            return 0

        lax.fori_loop(0, 4, finish, 0)
        if q == 0:
            go(full.at[pl.ds(2, 2)], full.at[pl.ds(10, 2)], rim_s, rim_r, 0, (before, c))
            go(full.at[pl.ds(4, 2)], full.at[pl.ds(0, 2)], rim_s, rim_r, 1, (after, c))
    remote(full.at[pl.ds(10, 2)], full.at[pl.ds(10, 2)], rim_s, rim_r, 0, (before, c)).wait_recv()
    remote(full.at[pl.ds(0, 2)], full.at[pl.ds(0, 2)], rim_s, rim_r, 1, (after, c)).wait_recv()

    def state_of(b):
        r = rev[b]
        holder, within = r // EB, r % EB
        at = jnp.where(holder == g, 2 + within, jnp.where(holder == before, within - 2, 10 + within))
        at = jnp.clip(at, 0, EB + 3)
        return (full[2 + b].astype(jnp.float32) + full[at].astype(jnp.float32)) * SCALE

    def theirs(i, _):
        give[i] = state_of((1 - c) * 4 + i)
        return 0

    lax.fori_loop(0, 4, theirs, 0)
    go(give, st.at[c], mp_s, mp_r, 2, partner)

    def mine(i, _):
        st[c, i] = state_of(c * 4 + i)
        return 0

    lax.fori_loop(0, 4, mine, 0)
    remote(win2, win2, mp_s, mp_r, 0, partner).wait_recv()
    remote(wout2, wout2, mp_s, mp_r, 1, partner).wait_recv()
    remote(st.at[1 - c], st.at[1 - c], mp_s, mp_r, 2, partner).wait_recv()

    def silu(v):
        h = v * 0.5
        return h + h * jnp.tanh(h)

    def mm(a, b):
        return jnp.dot(a, b, preferred_element_type=jnp.float32)

    def layer(k, _):
        xin = jnp.concatenate([st[n].reshape(512, 256).astype(jnp.bfloat16) for n in (0, 1)], axis=1)
        hid[0] = silu(mm(xin, w_in[k])).astype(jnp.bfloat16)
        hid[1] = silu(mm(xin, win2[k])).astype(jnp.bfloat16)
        for n in (0, 1):
            cols = pl.ds(n * 256, 256)
            step = mm(hid[0], w_out[k, :, cols]) + mm(hid[1], wout2[k, :, cols])
            st[n] = st[n] + step.reshape(4, BLK, 256)
        return 0

    lax.fori_loop(0, MLPS, layer, 0)
    row = lax.broadcasted_iota(jnp.int32, (512, 256), 0) + c * 512
    for n in (0, 1):
        res[n] = jnp.where(row < valid[0], st[n].reshape(512, 256), 0.0).astype(jnp.bfloat16)
    go(res.at[1 - c], fin, mp_s, mp_r, 3, partner)
    out[pl.ds(c * 512, 512)] = res[c]
    remote(fin, fin, mp_s, mp_r, 3, partner).wait_recv()
    out[pl.ds((1 - c) * 512, 512)] = fin[...]
    for cp in started:
        cp.wait_send()


def tail(rev, valid, part, messages, w_in, w_out):
    rows, width = messages.shape
    vm = pl.BlockSpec(memory_space=VMEM)
    smem = pl.BlockSpec(memory_space=SMEM)
    dma = pltpu.SemaphoreType.DMA
    bf, f32 = jnp.bfloat16, jnp.float32
    chunk = (4, EB, BLK, width)
    return pl.pallas_call(
        tail_kernel,
        out_shape=jax.ShapeDtypeStruct((rows, width), bf),
        in_specs=[smem, smem, vm, vm, vm, vm],
        out_specs=vm,
        scratch_shapes=[
            VMEM(chunk, bf), VMEM(chunk, bf), VMEM(chunk, bf), VMEM(chunk, bf),
            VMEM((EB + 4, BLK, width), bf),
            VMEM((2, 4, BLK, width), f32),
            VMEM((4, BLK, width), f32),
            VMEM(w_in.shape, bf), VMEM(w_out.shape, bf),
            VMEM((2, rows // 2, width), bf),
            VMEM((2, rows // 2, width), bf),
            VMEM((rows // 2, width), bf),
            dma((16,)), dma((16,)), dma((2,)), dma((2,)), dma((4,)), dma((4,)),
        ],
        compiler_params=pltpu.CompilerParams(collective_id=1, has_side_effects=True),
        name="tail",
    )(rev, valid, part, messages.reshape(EB, BLK, width), w_in, w_out)


def local(
    messages, basis_blocks, source_block, target_owner, target_block,
    row_counts, reverse_block, valid_edges, weight_in, weight_out,
):
    core = lax.axis_index("mp").reshape(1)
    slots, meta = slot_blocks(core, target_owner[:, 0], source_block, target_block, row_counts, basis_blocks)
    gathered, basis, metas = plane_exchange(messages, slots, meta)
    part = plane_products(metas, gathered, basis)
    return tail(reverse_block, valid_edges, part, messages, weight_in, weight_out)


def solution(mesh):
    in_specs = (
        P("graph", "mp"),
        P("graph", None, None),
        P("graph"),
        P("graph", None),
        P("graph"),
        P("graph"),
        P("graph"),
        P("graph"),
        P(None, None, "mp"),
        P(None, "mp", None),
    )
    return jax.shard_map(local, mesh=mesh, in_specs=in_specs, out_specs=P("graph", "mp"), check_vma=False)
```

time: 638 us -> 213 us (0.33)
  waiting for transfers between devices: 464 us -> 0 us
  Pallas kernels: 0 us -> 208 us
  local copies, waits for them, and re-layouts: 83.3 us -> 1.87 us
  starting transfers between devices: 32.1 us -> 0 us
  matrix products: 29.3 us -> 0 us
  between operations: 14.3 us -> 0.68 us
  other arithmetic: 13.6 us -> 0 us
    all_to_all x2 -> x0, waiting for transfers between devices: 364 us -> none  [the longest x1 364 us: local(): lax.all_to_all(out_products, 'graph', split_axis=0, concat_axis=0, tiled=...]
    pallas_call x0 -> x4, Pallas kernels: none -> 208 us  [the longest x1 106 us: plane_exchange(): pl.pallas_call(plane_kernel, out_shape=(jax.ShapeDtypeStruct((PLANE,) + m...]
    reduce_scatter x3 -> x0, waiting for transfers between devices: 47.5 us -> none  [local(): lax.psum_scatter(partial_sum, 'mp', scatter_dimension=1, tiled=True)]
    all_gather x3 -> x0, waiting for transfers between devices: 42.6 us -> none  [local(): lax.all_gather(state.astype(jnp.bfloat16), 'mp', axis=1, tiled=True)]
    all_to_all x2 -> x0, starting transfers between devices: 30.1 us -> none  [the longest x1 16.3 us: local(): lax.all_to_all(out_labels, 'graph', split_axis=0, concat_axis=0, tiled=True)]
    dot_general x5 -> x0, matrix products: 29.3 us -> none  [the longest x3 11.3 us: local(): jnp.dot(hidden, weight_out[layer], preferred_element_type=jnp.float32)]
    dot_general x1 -> x0, local copies, waits for them, and re-layouts: 22.3 us -> none  [sum_into_blocks(): jnp.dot(selector, incoming.reshape(count_all, rows * cols), preferred_ele...]
    scatter x2 -> x0, local copies, waits for them, and re-layouts: 18.8 us -> none  [place_slots(): jnp.zeros((devices * capacity,) + shape_rest, values.dtype).at[place]]
  transfers between devices with their start and end apart: 10 -> 0, of which waited for: 9 -> 0; matrix products, arithmetic and copies ran while one was open for 8% -> 0% of each run, Pallas kernels for 0% -> 0%
where the time goes in v1:
time: 213 us; the launch traced here: 210 us
  Pallas kernels  208 us (98%)
    pallas_call x1, Pallas kernels, plane_exchange(): pl.pallas_call(plane_kernel, out_shape=(jax.ShapeDtypeStruct((PLANE,) + m...  106 us
    pallas_call x1, Pallas kernels, tail(): pl.pallas_call(tail_kernel, out_shape=jax.ShapeDtypeStruct((rows, width),...  63.2 us
    pallas_call x1, Pallas kernels, plane_products(): pl.pallas_call(product_kernel, out_shape=jax.ShapeDtypeStruct((NZ * EB, B...  30.4 us
    pallas_call x1, Pallas kernels, slot_blocks(): pl.pallas_call(slot_kernel, out_shape=(jax.ShapeDtypeStruct((PLANE * NZ,...  8.38 us

profile of v1, /device:TPU:1, one launch (start us, length us, event | category | flops | bytes accessed | tf_op | source)
XLA Modules:
  0.0 210.3 jit_solution(13004425531678370837)
XLA Ops:
  0.0 8.4 %slots.1 = (bf16[128,128,128]{2,1,0:T(8,128)(2,1)}, s32[16,8,128]{2,1,0:T(8,128)}) custom-call(s32[1]{0:T(128)} %bitcast.core_ref, s32[96]{0:T(128)} %bitcast.6, s32[96]{0:T(128)} %source_ref.1, s32[96]{0:T(128)} %target_ref.1, s32[96]{0:T(128)} %count_ref.1, bf16[96,128,128]{2,1,0:T(8,128)(2,1)} %basis_ref.1), custom_call_target="tpu_custom_call" | custom-call | tf_op jit(solution)/shard_map/slots/pallas_call | solution.py:57
  8.4 105.7 %plane.1 = (bf16[16,1024,256]{2,1,0:T(8,128)(2,1)}, bf16[2,16,8,128,128]{4,3,2,1,0:T(8,128)(2,1)}, s32[16,8,128]{2,1,0:T(8,128)}) custom-call(bf16[1024,256]{1,0:T(8,128)(2,1)} %msg.1, bf16[128,128,128]{2,1,0:T(8,128)(2,1)} %get-tuple-element.10.pb, s32[16,8,128]{2,1,0:T(8,128)} %get-tuple-element.11.meta), custom_call_target="tpu_custom_call" | custom-call | tf_op jit(solution)/shard_map/plane/pallas_call | solution.py:243
  114.1 30.4 %products.1.part = bf16[64,128,256]{2,1,0:T(8,128)(2,1)} custom-call(s32[16,8,128]{2,1,0:T(8,128)} %get-tuple-element.12.meta, bf16[16,8,128,256]{3,2,1,0:T(8,128)(2,1)} %bitcast.4, bf16[2,16,8,128,128]{4,3,2,1,0:T(8,128)(2,1)} %get-tuple-element.14.b_ref), custom_call_target="tpu_custom_call" | custom-call | tf_op jit(solution)/shard_map/products/pallas_call | solution.py:288
  145.2 63.2 %tail.1 = bf16[1024,256]{1,0:T(8,128)(2,1)} custom-call(s32[8]{0:T(128)} %rev.1, s32[1]{0:T(128)S(6)} %copy.12.valid, bf16[64,128,256]{2,1,0:T(8,128)(2,1)} %products.1.part, bf16[8,128,256]{2,1,0:T(8,128)(2,1)} %bitcast.5, bf16[3,512,256]{2,1,0:T(8,128)(2,1)} %w_in.1, bf16[3,256,512]{2,1,0:T(8,128)(2,1)} %w_out.1), custom_call_target="tpu_custom_call" | custom-call | tf_op jit(solution)/shard_map/tail/pallas_call | solution.py:454
  208.4 1.9 copy.13
